TPU v7x, 256 devices: a whole 4x4x8 slice. The times are simulated.
256 devices in a mesh: row: 16 (over z_lo, y, core), col: 16 (over x, z_hi).
Axes of the slice: x: 4, y: 4, z: 8 (z_hi: 4, z_lo: 2; z = z_hi * 2 + z_lo), core: 2. Of those that a mesh axis runs over, the one named last changes fastest.
Arguments:
- positions: float32 [3, 262144], P(None, ('col', 'row')), may hold values from 0 to 16
- velocity: float32 [3, 262144], P(None, ('col', 'row')), may hold values from -6 to 6
- applied: float32 [3, 262144], P(None, ('col', 'row')), may hold values from -12 to 12
- suscept: float32 [262144], P(('col', 'row')), may hold values from 0.05 to 0.3
- contact_owner: int32 [16, 16, 16, 512], P('col', 'row'), may hold values from 0 to 1023
- contact_partner: int32 [16, 16, 16, 512], P('col', 'row'), may hold values from 0 to 1023
- contact_count: int32 [16, 16, 16], P('col', 'row'), may hold values from 1 to 512, as said below
Outputs:
- moments: float32 [3, 262144], P(None, ('col', 'row'))
- forces: float32 [3, 262144], P(None, ('col', 'row'))
Inputs may be any that keep to these rules, and one draw needn't show every extreme that they name: `contact_count`: in every draw one column receives full blocks of 512 live slots from every device; the other columns' blocks are filled to different depths.
All inputs are finite; a program needn't handle non-finite values.
Results may differ from a plain program's by a relative error of at most 0.0003.
Values sent between devices are 32-bit elements; how exact they have to be, the bound alone decides.
A program may use at most 64 MiB of HBM per device.

v0:
```python
import math
import jax
import jax.numpy as jnp
from jax import lax
from jax.sharding import PartitionSpec as P

ITERS = 2


def dipole_block(target_pos, target_ids, source_pos, source_mom, source_ids):
    offset = target_pos[:, :, None] - source_pos[:, None, :]
    radius_sq = jnp.sum(offset * offset, axis=0) + 1.0
    inverse_r = lax.rsqrt(radius_sq)
    inverse_cube = inverse_r * inverse_r * inverse_r
    inverse_fifth = inverse_cube * inverse_r * inverse_r
    keep_mask = target_ids[:, None] != source_ids[None, :]
    projection = jnp.sum(offset * source_mom[:, None, :], axis=0)
    radial_coef = jnp.where(keep_mask, 3.0 * projection * inverse_fifth, 0.0)
    direct_coef = jnp.where(keep_mask, inverse_cube, 0.0)
    return jnp.sum(radial_coef[None] * offset, axis=2) - jnp.sum(
        direct_coef[None] * source_mom[:, None, :], axis=2
    )


def local_field(target_pos, target_ids, source_pos, source_mom, source_ids):
    target_len = target_pos.shape[1]
    source_len = source_pos.shape[1]
    target_block = math.gcd(target_len, 128)
    source_block = math.gcd(source_len, 512)
    target_count = target_len // target_block
    source_count = source_len // source_block
    source_blocks = (
        source_pos.reshape(3, source_count, source_block).transpose(1, 0, 2),
        source_mom.reshape(3, source_count, source_block).transpose(1, 0, 2),
        source_ids.reshape(source_count, source_block),
    )
    target_blocks = (
        target_pos.reshape(3, target_count, target_block).transpose(1, 0, 2),
        target_ids.reshape(target_count, target_block),
    )

    def per_target(target_pair):

        def add_block(field_sum, source_triple):
            return (
                field_sum
                + dipole_block(
                    target_pair[0],
                    target_pair[1],
                    source_triple[0],
                    source_triple[1],
                    source_triple[2],
                ),
                None,
            )

        field_sum, unused = lax.scan(
            add_block, jnp.zeros((3, target_block), jnp.float32), source_blocks
        )
        return field_sum

    result_blocks = lax.map(per_target, target_blocks)
    return result_blocks.transpose(1, 0, 2).reshape(3, target_len)


def pair_force(one_side, other_side):
    separation = one_side[0:3] - other_side[0:3]
    distance = jnp.sqrt(jnp.sum(separation * separation, axis=0) + 1.0)
    normal = separation / distance
    mom_one = one_side[6:9]
    mom_other = other_side[6:9]
    along_one = jnp.sum(mom_one * normal, axis=0)
    along_other = jnp.sum(mom_other * normal, axis=0)
    mom_dot = jnp.sum(mom_one * mom_other, axis=0)
    magnetic = 3.0 * (
        along_one * mom_other
        + along_other * mom_one
        + (mom_dot - 5.0 * along_one * along_other) * normal
    )
    spring = -0.03 * (distance - 1.0) * normal
    rel_speed = jnp.sum((one_side[3:6] - other_side[3:6]) * normal, axis=0)
    damping = -0.5 * rel_speed * normal
    return magnetic + spring + damping


def accumulate(slot_values, slot_ids, particle_count):
    flat_ids = slot_ids.reshape(-1)
    flat_values = slot_values.reshape(3, -1)
    return jnp.zeros((3, particle_count), jnp.float32).at[:, flat_ids].add(flat_values)


def on_device(positions, velocity, applied, suscept, contact_owner, contact_partner, contact_count):
    particle_count = positions.shape[1]
    row_index = lax.axis_index("row")
    own_ids = row_index * particle_count + jnp.arange(particle_count, dtype=jnp.int32)
    moments = suscept[None, :] * applied
    for iteration in range(ITERS):
        shard_pieces = (
            lax.all_gather(positions, "row", axis=1, tiled=True),
            lax.all_gather(moments, "row", axis=1, tiled=True),
        )
        piece_len = shard_pieces[0].shape[1]
        source_ids = jnp.arange(piece_len, dtype=jnp.int32)
        field_sum = local_field(positions, own_ids, shard_pieces[0], shard_pieces[1], source_ids)
        moments = suscept[None, :] * (applied + field_sum)
    col_count = contact_owner.shape[2]
    slot_count = contact_owner.shape[3]
    owner_ids = contact_owner.reshape(col_count, slot_count)
    partner_ids = contact_partner.reshape(col_count, slot_count)
    count_here = contact_count.reshape(col_count)
    live_mask = (jnp.arange(slot_count, dtype=jnp.int32)[None, :] < count_here[:, None]).astype(
        jnp.float32
    )
    state_rows = jnp.concatenate([positions, velocity, moments], axis=0)
    owner_rows = jnp.take(state_rows, owner_ids, axis=1)
    asked_ids = lax.all_to_all(partner_ids, "col", split_axis=0, concat_axis=0, tiled=True)
    looked_up = jnp.take(state_rows, asked_ids, axis=1)
    sent_rows = lax.all_to_all(looked_up, "col", split_axis=1, concat_axis=1, tiled=True)
    partner_rows, asked_ids = (sent_rows, asked_ids[None])
    slot_force = pair_force(owner_rows, partner_rows) * live_mask[None]
    owner_force = accumulate(slot_force, owner_ids, particle_count)
    returned = lax.all_to_all(slot_force, "col", split_axis=1, concat_axis=1, tiled=True)
    forces = owner_force - accumulate(returned, asked_ids[0], particle_count)
    return (moments, forces)


def solution(mesh):
    placed = (
        P(None, ("col", "row")),
        P(None, ("col", "row")),
        P(None, ("col", "row")),
        P(("col", "row")),
        P("col", "row", None, None),
        P("col", "row", None, None),
        P("col", "row", None),
    )
    return jax.shard_map(
        on_device,
        mesh=mesh,
        in_specs=placed,
        out_specs=(P(None, ("col", "row")), P(None, ("col", "row"))),
        check_vma=False,
    )
```

profile of v0, /device:TPU:1, one launch (start us, length us, event | category | flops | bytes accessed | tf_op | source)
XLA Modules:
  0.0 661.3 jit_solution(5421907334864235557)
XLA Ops:
  2.0 11.6 %all-to-all-start = ((s32[16,1,512]{2,1,0:T(1,128)}), s32[16,1,512]{2,1,0:T(1,128)S(1)}, u32[]{:S(2)}, u32[]{:S(2)}) async-start(s32[16,1,512]{2,1,0:T(1,128)} %all_to_all.14), calls=%async_computation | async-start | bytes 65536 | tf_op jit(solution)/shard_map/all_to_all | solution.py:116
  15.2 21.1 %all_gather.10 = f32[3,16384]{1,0:T(4,128)S(1)} all-gather(f32[3,1024]{1,0:T(4,128)} %param.17), channel_id=1, replica_groups=mesh['row'=16,'col'=16] {'row'}, dimensions={1}, use_global_device_ids=true | all-gather | bytes 208896 | tf_op jit(solution)/shard_map/all_gather | solution.py:99
  37.0 17.0 %all_gather.11 = f32[3,16384]{1,0:T(4,128)S(1)} all-gather(f32[3,1024]{1,0:T(4,128)S(1)} %broadcast_multiply_fusion.1), channel_id=1, replica_groups=mesh['row'=16,'col'=16] {'row'}, dimensions={1}, use_global_device_ids=true | all-gather | bytes 208896 | tf_op jit(solution)/shard_map/all_gather | solution.py:100
  54.0 204.9 %while.47 = (s32[]{:T(128)}, f32[8,3,128]{2,1,0:T(4,128)S(1)}, f32[8,3,128]{2,1,0:T(4,128)}, s32[8,128]{1,0:T(8,128)S(1)}, f32[32,3,512]{2,1,0:T(4,128)S(1)}, /*...) while((s32[]{:T(128)}, f32[8,3,128]{2,1,0:T(4,128)S(1)}, ...), condition=%wide.region_7.8_spmd.clone, body=%wide.region_0.7_spmd.clone.sunk | while | flops 2523525 | bytes 2239280 | solution.py:62
  54.7 24.9 %while.50 = (s32[]{:T(128)}, f32[3,128]{1,0:T(4,128)S(1)}, s32[128]{0:T(128)S(1)}, s32[32,512]{1,0:T(8,128)S(1)}, f32[3,128]{1,0:T(4,128)S(1)}, /*index=5*/f32[3...) while((s32[]{:T(128)}, f32[3,128]{1,0:T(4,128)S(1)}, s32[128]{0:T(128)S(1)}, ...), condition=%wide.region_6.6_spmd.clone, body=%wide.region_1.5_spmd.clone.sunk | while | flops 2490755 | bytes 2165359 | solution.py:57
  80.3 24.9 %while.50 = (s32[]{:T(128)}, f32[3,128]{1,0:T(4,128)S(1)}, s32[128]{0:T(128)S(1)}, s32[32,512]{1,0:T(8,128)S(1)}, f32[3,128]{1,0:T(4,128)S(1)}, /*index=5*/f32[3...) while((s32[]{:T(128)}, f32[3,128]{1,0:T(4,128)S(1)}, s32[128]{0:T(128)S(1)}, ...), condition=%wide.region_6.6_spmd.clone, body=%wide.region_1.5_spmd.clone.sunk | while | flops 2490755 | bytes 2165359 | solution.py:57
  105.9 24.9 %while.50 = (s32[]{:T(128)}, f32[3,128]{1,0:T(4,128)S(1)}, s32[128]{0:T(128)S(1)}, s32[32,512]{1,0:T(8,128)S(1)}, f32[3,128]{1,0:T(4,128)S(1)}, /*index=5*/f32[3...) while((s32[]{:T(128)}, f32[3,128]{1,0:T(4,128)S(1)}, s32[128]{0:T(128)S(1)}, ...), condition=%wide.region_6.6_spmd.clone, body=%wide.region_1.5_spmd.clone.sunk | while | flops 2490755 | bytes 2165359 | solution.py:57
  131.5 24.9 %while.50 = (s32[]{:T(128)}, f32[3,128]{1,0:T(4,128)S(1)}, s32[128]{0:T(128)S(1)}, s32[32,512]{1,0:T(8,128)S(1)}, f32[3,128]{1,0:T(4,128)S(1)}, /*index=5*/f32[3...) while((s32[]{:T(128)}, f32[3,128]{1,0:T(4,128)S(1)}, s32[128]{0:T(128)S(1)}, ...), condition=%wide.region_6.6_spmd.clone, body=%wide.region_1.5_spmd.clone.sunk | while | flops 2490755 | bytes 2165359 | solution.py:57
  157.2 24.9 %while.50 = (s32[]{:T(128)}, f32[3,128]{1,0:T(4,128)S(1)}, s32[128]{0:T(128)S(1)}, s32[32,512]{1,0:T(8,128)S(1)}, f32[3,128]{1,0:T(4,128)S(1)}, /*index=5*/f32[3...) while((s32[]{:T(128)}, f32[3,128]{1,0:T(4,128)S(1)}, s32[128]{0:T(128)S(1)}, ...), condition=%wide.region_6.6_spmd.clone, body=%wide.region_1.5_spmd.clone.sunk | while | flops 2490755 | bytes 2165359 | solution.py:57
  182.8 24.9 %while.50 = (s32[]{:T(128)}, f32[3,128]{1,0:T(4,128)S(1)}, s32[128]{0:T(128)S(1)}, s32[32,512]{1,0:T(8,128)S(1)}, f32[3,128]{1,0:T(4,128)S(1)}, /*index=5*/f32[3...) while((s32[]{:T(128)}, f32[3,128]{1,0:T(4,128)S(1)}, s32[128]{0:T(128)S(1)}, ...), condition=%wide.region_6.6_spmd.clone, body=%wide.region_1.5_spmd.clone.sunk | while | flops 2490755 | bytes 2165359 | solution.py:57
  208.4 24.9 %while.50 = (s32[]{:T(128)}, f32[3,128]{1,0:T(4,128)S(1)}, s32[128]{0:T(128)S(1)}, s32[32,512]{1,0:T(8,128)S(1)}, f32[3,128]{1,0:T(4,128)S(1)}, /*index=5*/f32[3...) while((s32[]{:T(128)}, f32[3,128]{1,0:T(4,128)S(1)}, s32[128]{0:T(128)S(1)}, ...), condition=%wide.region_6.6_spmd.clone, body=%wide.region_1.5_spmd.clone.sunk | while | flops 2490755 | bytes 2165359 | solution.py:57
  234.0 24.9 %while.50 = (s32[]{:T(128)}, f32[3,128]{1,0:T(4,128)S(1)}, s32[128]{0:T(128)S(1)}, s32[32,512]{1,0:T(8,128)S(1)}, f32[3,128]{1,0:T(4,128)S(1)}, /*index=5*/f32[3...) while((s32[]{:T(128)}, f32[3,128]{1,0:T(4,128)S(1)}, s32[128]{0:T(128)S(1)}, ...), condition=%wide.region_6.6_spmd.clone, body=%wide.region_1.5_spmd.clone.sunk | while | flops 2490755 | bytes 2165359 | solution.py:57
  258.9 18.3 %all_gather.12 = f32[3,16384]{1,0:T(4,128)S(1)} all-gather(f32[3,1024]{1,0:T(4,128)S(1)} %fusion.26), channel_id=1, replica_groups=mesh['row'=16,'col'=16] {'row'}, dimensions={1}, use_global_device_ids=true | all-gather | bytes 208896 | tf_op jit(solution)/shard_map/all_gather | solution.py:100
  277.2 204.9 %while.49 = (s32[]{:T(128)}, f32[8,3,128]{2,1,0:T(4,128)S(1)}, f32[8,3,128]{2,1,0:T(4,128)}, s32[8,128]{1,0:T(8,128)S(1)}, f32[32,3,512]{2,1,0:T(4,128)S(1)}, /*...) while((s32[]{:T(128)}, f32[8,3,128]{2,1,0:T(4,128)S(1)}, ...), condition=%wide.region_15.16_spmd.clone, body=%wide.region_8.15_spmd.clone.sunk | while | flops 2523525 | bytes 2239280 | solution.py:62
  278.0 24.9 %while.51 = (s32[]{:T(128)}, f32[3,128]{1,0:T(4,128)S(1)}, s32[128]{0:T(128)S(1)}, s32[32,512]{1,0:T(8,128)S(1)}, f32[3,128]{1,0:T(4,128)S(1)}, /*index=5*/f32[3...) while((s32[]{:T(128)}, f32[3,128]{1,0:T(4,128)S(1)}, s32[128]{0:T(128)S(1)}, ...), condition=%wide.region_14.14_spmd.clone, body=%wide.region_9.13_spmd.clone.sunk | while | flops 2490755 | bytes 2165359 | solution.py:57
  303.6 24.9 %while.51 = (s32[]{:T(128)}, f32[3,128]{1,0:T(4,128)S(1)}, s32[128]{0:T(128)S(1)}, s32[32,512]{1,0:T(8,128)S(1)}, f32[3,128]{1,0:T(4,128)S(1)}, /*index=5*/f32[3...) while((s32[]{:T(128)}, f32[3,128]{1,0:T(4,128)S(1)}, s32[128]{0:T(128)S(1)}, ...), condition=%wide.region_14.14_spmd.clone, body=%wide.region_9.13_spmd.clone.sunk | while | flops 2490755 | bytes 2165359 | solution.py:57
  329.2 24.9 %while.51 = (s32[]{:T(128)}, f32[3,128]{1,0:T(4,128)S(1)}, s32[128]{0:T(128)S(1)}, s32[32,512]{1,0:T(8,128)S(1)}, f32[3,128]{1,0:T(4,128)S(1)}, /*index=5*/f32[3...) while((s32[]{:T(128)}, f32[3,128]{1,0:T(4,128)S(1)}, s32[128]{0:T(128)S(1)}, ...), condition=%wide.region_14.14_spmd.clone, body=%wide.region_9.13_spmd.clone.sunk | while | flops 2490755 | bytes 2165359 | solution.py:57
  354.8 24.9 %while.51 = (s32[]{:T(128)}, f32[3,128]{1,0:T(4,128)S(1)}, s32[128]{0:T(128)S(1)}, s32[32,512]{1,0:T(8,128)S(1)}, f32[3,128]{1,0:T(4,128)S(1)}, /*index=5*/f32[3...) while((s32[]{:T(128)}, f32[3,128]{1,0:T(4,128)S(1)}, s32[128]{0:T(128)S(1)}, ...), condition=%wide.region_14.14_spmd.clone, body=%wide.region_9.13_spmd.clone.sunk | while | flops 2490755 | bytes 2165359 | solution.py:57
  380.4 24.9 %while.51 = (s32[]{:T(128)}, f32[3,128]{1,0:T(4,128)S(1)}, s32[128]{0:T(128)S(1)}, s32[32,512]{1,0:T(8,128)S(1)}, f32[3,128]{1,0:T(4,128)S(1)}, /*index=5*/f32[3...) while((s32[]{:T(128)}, f32[3,128]{1,0:T(4,128)S(1)}, s32[128]{0:T(128)S(1)}, ...), condition=%wide.region_14.14_spmd.clone, body=%wide.region_9.13_spmd.clone.sunk | while | flops 2490755 | bytes 2165359 | solution.py:57
  406.0 24.9 %while.51 = (s32[]{:T(128)}, f32[3,128]{1,0:T(4,128)S(1)}, s32[128]{0:T(128)S(1)}, s32[32,512]{1,0:T(8,128)S(1)}, f32[3,128]{1,0:T(4,128)S(1)}, /*index=5*/f32[3...) while((s32[]{:T(128)}, f32[3,128]{1,0:T(4,128)S(1)}, s32[128]{0:T(128)S(1)}, ...), condition=%wide.region_14.14_spmd.clone, body=%wide.region_9.13_spmd.clone.sunk | while | flops 2490755 | bytes 2165359 | solution.py:57
  431.6 24.9 %while.51 = (s32[]{:T(128)}, f32[3,128]{1,0:T(4,128)S(1)}, s32[128]{0:T(128)S(1)}, s32[32,512]{1,0:T(8,128)S(1)}, f32[3,128]{1,0:T(4,128)S(1)}, /*index=5*/f32[3...) while((s32[]{:T(128)}, f32[3,128]{1,0:T(4,128)S(1)}, s32[128]{0:T(128)S(1)}, ...), condition=%wide.region_14.14_spmd.clone, body=%wide.region_9.13_spmd.clone.sunk | while | flops 2490755 | bytes 2165359 | solution.py:57
  457.2 24.9 %while.51 = (s32[]{:T(128)}, f32[3,128]{1,0:T(4,128)S(1)}, s32[128]{0:T(128)S(1)}, s32[32,512]{1,0:T(8,128)S(1)}, f32[3,128]{1,0:T(4,128)S(1)}, /*index=5*/f32[3...) while((s32[]{:T(128)}, f32[3,128]{1,0:T(4,128)S(1)}, s32[128]{0:T(128)S(1)}, ...), condition=%wide.region_14.14_spmd.clone, body=%wide.region_9.13_spmd.clone.sunk | while | flops 2490755 | bytes 2165359 | solution.py:57
  483.3 27.7 %gather_fusion.1 = f32[8192,9]{1,0:T(8,128)} fusion(f32[9,1024]{0,1:T(8,128)S(1)} %copy.38, s32[8192]{0:T(1024)S(1)} %broadcast_clamp_fusion), kind=kCustom, calls=%fused_computation.1.clone | custom fusion | bytes 622592 | tf_op jit(solution)/shard_map/jit(_take)/gather | solution.py:117
  511.0 2.8 copy.41
  514.7 9.5 %all-to-all-start.1 = ((f32[9,16,512]{2,0,1:T(8,128)}), f32[9,16,512]{2,0,1:T(8,128)S(1)}, u32[]{:S(2)}, u32[]{:S(2)}) async-start(f32[9,16,512]{2,0,1:T(8,128)} %select_bitcast_fusion), calls=%async_computation.1 | async-start | bytes 1048576 | tf_op jit(solution)/shard_map/all_to_all | solution.py:118
  524.3 27.7 %gather_fusion = f32[8192,9]{1,0:T(8,128)} fusion(f32[9,1024]{0,1:T(8,128)S(1)} %copy.38, s32[8192]{0:T(1024)S(1)} %broadcast_clamp_fusion.1), kind=kCustom, calls=%fused_computation.clone | custom fusion | bytes 622592 | tf_op jit(solution)/shard_map/jit(_take)/gather | solution.py:115
  552.0 2.8 copy.39
  556.4 9.1 %all-to-all-start.2 = ((f32[3,16,512]{2,0,1:T(4,128)}), f32[3,16,512]{2,0,1:T(4,128)S(1)}, u32[]{:S(2)}, u32[]{:S(2)}) async-start(f32[3,16,512]{2,0,1:T(4,128)} %add_multiply_fusion), calls=%async_computation.2 | async-start | bytes 262144 | tf_op jit(solution)/shard_map/all_to_all | solution.py:122
  565.5 3.4 copy.42
  569.0 44.4 %scatter_custom_fusion = f32[3,1024]{0,1:T(8,128)S(1)} fusion(s32[8192]{0:T(1024)S(1)} %bitcast.120, f32[8192,3]{1,0:T(8,128)} %copy.42, f32[]{:T(128)} %constant.84.clone.1), kind=kCustom, calls=%fused_computation.54 | custom fusion | flops 24576 | bytes 12800 | tf_op jit(solution)/shard_map/scatter-add | solution.py:89
  613.4 2.6 copy.43
  616.0 44.4 %scatter_custom_fusion.1 = f32[3,1024]{0,1:T(8,128)S(1)} fusion(s32[8192]{0:T(1024)S(1)} %bitcast.121, f32[8192,3]{1,0:T(8,128)} %copy.43, f32[]{:T(128)} %constant.84.clone.1), kind=kCustom, calls=%fused_computation.52 | custom fusion | flops 24576 | bytes 12800 | tf_op jit(solution)/shard_map/scatter-add | solution.py:89
  (3709 shorter events, 392.6 us)
Async XLA Ops:
  2.0 481.2 %all-to-all-start = ((s32[16,1,512]{2,1,0:T(1,128)}), s32[16,1,512]{2,1,0:T(1,128)S(1)}, u32[]{:S(2)}, u32[]{:S(2)}) async-start(s32[16,1,512]{2,1,0:T(1,128)} %all_to_all.14), calls=%async_computation | async-start | bytes 65536 | tf_op jit(solution)/shard_map/all_to_all | solution.py:116
  54.0 204.9 %copy-start.1 = (f32[3,1024]{1,0:T(4,128)S(1)}, f32[3,1024]{1,0:T(4,128)}, u32[]{:S(2)}) copy-start(f32[3,1024]{1,0:T(4,128)} %param.19) | copy-start | bytes 36868
  54.0 204.9 %copy-start.3 = (f32[1024]{0:T(1024)S(1)}, f32[1024]{0:T(1024)}, u32[]{:S(2)}) copy-start(f32[1024]{0:T(1024)} %param.20) | copy-start | bytes 12292
  277.2 205.0 %copy-start.4 = (f32[3,1024]{1,0:T(4,128)S(1)}, f32[3,1024]{1,0:T(4,128)}, u32[]{:S(2)}) copy-start(f32[3,1024]{1,0:T(4,128)} %param.18) | copy-start | bytes 36868
  482.1 31.7 %copy-start.2 = (f32[3,1024]{1,0:T(4,128)}, f32[3,1024]{1,0:T(4,128)S(1)}, u32[]{:S(2)}) copy-start(f32[3,1024]{1,0:T(4,128)S(1)} %fusion.25) | copy-start | bytes 36868
  483.3 40.9 %copy-start.5 = (s32[1,1,16]{2,1,0:T(1,128)S(1)}, s32[1,1,16]{2,1,0:T(1,128)}, u32[]{:S(2)}) copy-start(s32[1,1,16]{2,1,0:T(1,128)} %param.23) | copy-start | bytes 196
  514.7 40.1 %copy-start = (s32[1,1,16,512]{3,2,1,0:T(8,128)S(1)}, s32[1,1,16,512]{3,2,1,0:T(8,128)}, u32[]{:S(2)}) copy-start(s32[1,1,16,512]{3,2,1,0:T(8,128)} %param.21) | copy-start | bytes 98308
  514.7 40.2 %all-to-all-start.1 = ((f32[9,16,512]{2,0,1:T(8,128)}), f32[9,16,512]{2,0,1:T(8,128)S(1)}, u32[]{:S(2)}, u32[]{:S(2)}) async-start(f32[9,16,512]{2,0,1:T(8,128)} %select_bitcast_fusion), calls=%async_computation.1 | async-start | bytes 1048576 | tf_op jit(solution)/shard_map/all_to_all | solution.py:118
  556.4 57.0 %all-to-all-start.2 = ((f32[3,16,512]{2,0,1:T(4,128)}), f32[3,16,512]{2,0,1:T(4,128)S(1)}, u32[]{:S(2)}, u32[]{:S(2)}) async-start(f32[3,16,512]{2,0,1:T(4,128)} %add_multiply_fusion), calls=%async_computation.2 | async-start | bytes 262144 | tf_op jit(solution)/shard_map/all_to_all | solution.py:122
where the time goes:
time: 663 us; the launch traced here: 661 us
  other arithmetic  455 us (69%)
  local copies, waits for them, and re-layouts  93.3 us (14%)
  blocking collectives  56.4 us (9%)
  starting transfers between devices  30.1 us (5%)
  loops' own time  25.3 us (4%)
    reduce_sum x512, other arithmetic, dipole_block(): jnp.sum(radial_coef[None] * offset, axis=2)  126 us
    reduce_sum x512, other arithmetic, dipole_block(): radius_sq = jnp.sum(offset * offset, axis=0) + 1.0  97 us
    scatter-add x2, other arithmetic, accumulate(): jnp.zeros((3, particle_count), jnp.float32).at[:, flat_ids].add(flat_values)  88.9 us
    reduce_sum x512, other arithmetic, dipole_block(): jnp.sum(direct_coef[None] * source_mom[:, None, :], axis=2)  76.8 us
    select_n x512, other arithmetic, dipole_block(): direct_coef = jnp.where(keep_mask, inverse_cube, 0.0)  54.2 us
    all_gather x2, blocking collectives, on_device(): lax.all_gather(moments, 'row', axis=1, tiled=True)  35.3 us
    gather x2, local copies, waits for them, and re-layouts, on_device(): looked_up = jnp.take(state_rows, asked_ids, axis=1)  30.5 us
    gather x2, local copies, waits for them, and re-layouts, on_device(): owner_rows = jnp.take(state_rows, owner_ids, axis=1)  30.5 us
  transfers between devices with their start and end apart: 3, of which 0 were waited for; matrix products, arithmetic and copies ran while one was open for 71% of the time, Pallas kernels for 0%

commit v1 on v0

--- a/solution.py
+++ b/solution.py
@@ -5,6 +5,11 @@
 from jax.sharding import PartitionSpec as P
 
 ITERS = 2
+
+
+def gathered_along(x, mesh_axis, dim):
+    blocks = lax.all_gather(x, mesh_axis)
+    return jnp.concatenate(blocks, axis=dim)
 
 
 def dipole_block(target_pos, target_ids, source_pos, source_mom, source_ids):
@@ -97,7 +102,7 @@
     for iteration in range(ITERS):
         shard_pieces = (
             lax.all_gather(positions, "row", axis=1, tiled=True),
-            lax.all_gather(moments, "row", axis=1, tiled=True),
+            gathered_along(moments, "row", 1),
         )
         piece_len = shard_pieces[0].shape[1]
         source_ids = jnp.arange(piece_len, dtype=jnp.int32)

time: 663 us -> 663 us (level)
  no operation moved by 1% of the time
where the time goes in v1:
time: 663 us; the launch traced here: 661 us
  other arithmetic  455 us (69%)
  local copies, waits for them, and re-layouts  93.3 us (14%)
  blocking collectives  56.4 us (9%)
  starting transfers between devices  30.1 us (5%)
  loops' own time  25.3 us (4%)
    reduce_sum x512, other arithmetic, dipole_block(): jnp.sum(radial_coef[None] * offset, axis=2)  126 us
    reduce_sum x512, other arithmetic, dipole_block(): radius_sq = jnp.sum(offset * offset, axis=0) + 1.0  97 us
    scatter-add x2, other arithmetic, accumulate(): jnp.zeros((3, particle_count), jnp.float32).at[:, flat_ids].add(flat_values)  88.9 us
    reduce_sum x512, other arithmetic, dipole_block(): jnp.sum(direct_coef[None] * source_mom[:, None, :], axis=2)  76.8 us
    select_n x512, other arithmetic, dipole_block(): direct_coef = jnp.where(keep_mask, inverse_cube, 0.0)  54.2 us
    all_gather x2, blocking collectives, gathered_along(): blocks = lax.all_gather(x, mesh_axis)  35.3 us
    gather x2, local copies, waits for them, and re-layouts, on_device(): looked_up = jnp.take(state_rows, asked_ids, axis=1)  30.5 us
    gather x2, local copies, waits for them, and re-layouts, on_device(): owner_rows = jnp.take(state_rows, owner_ids, axis=1)  30.5 us
  transfers between devices with their start and end apart: 3, of which 0 were waited for; matrix products, arithmetic and copies ran while one was open for 71% of the time, Pallas kernels for 0%

profile of v1, /device:TPU:1, one launch (start us, length us, event | category | flops | bytes accessed | tf_op | source)
XLA Modules:
  0.0 661.3 jit_solution(4805045142621232272)
XLA Ops:
  2.0 11.6 %all-to-all-start = ((s32[16,1,512]{2,1,0:T(1,128)}), s32[16,1,512]{2,1,0:T(1,128)S(1)}, u32[]{:S(2)}, u32[]{:S(2)}) async-start(s32[16,1,512]{2,1,0:T(1,128)} %all_to_all.14), calls=%async_computation | async-start | bytes 65536 | tf_op jit(solution)/shard_map/all_to_all | solution.py:121
  15.2 21.1 %all_gather.16 = f32[3,16384]{1,0:T(4,128)S(1)} all-gather(f32[3,1024]{1,0:T(4,128)} %param.17), channel_id=1, replica_groups=mesh['row'=16,'col'=16] {'row'}, dimensions={1}, use_global_device_ids=true | all-gather | bytes 208896 | tf_op jit(solution)/shard_map/all_gather | solution.py:104
  37.0 17.0 %all-gather.2 = f32[16,3,1024]{2,1,0:T(4,128)S(1)} all-gather(f32[1,3,1024]{2,1,0:T(4,128)S(1)} %multiply_bitcast_fusion), channel_id=2, replica_groups=mesh['row'=16,'col'=16] {'row'}, dimensions={0}, use_global_device_ids=true | all-gather | bytes 208896 | tf_op jit(solution)/shard_map/all_gather | solution.py:11
  54.0 204.9 %while.47 = (s32[]{:T(128)}, f32[8,3,128]{2,1,0:T(4,128)S(1)}, f32[8,3,128]{2,1,0:T(4,128)}, s32[8,128]{1,0:T(8,128)S(1)}, f32[32,3,512]{2,1,0:T(4,128)S(1)}, /*...) while((s32[]{:T(128)}, f32[8,3,128]{2,1,0:T(4,128)S(1)}, ...), condition=%wide.region_7.8_spmd.clone, body=%wide.region_0.7_spmd.clone.sunk | while | flops 2523525 | bytes 2239280 | solution.py:67
  54.7 24.9 %while.50 = (s32[]{:T(128)}, f32[3,128]{1,0:T(4,128)S(1)}, s32[128]{0:T(128)S(1)}, s32[32,512]{1,0:T(8,128)S(1)}, f32[3,128]{1,0:T(4,128)S(1)}, /*index=5*/f32[3...) while((s32[]{:T(128)}, f32[3,128]{1,0:T(4,128)S(1)}, s32[128]{0:T(128)S(1)}, ...), condition=%wide.region_6.6_spmd.clone, body=%wide.region_1.5_spmd.clone.sunk | while | flops 2490755 | bytes 2165359 | solution.py:62
  80.3 24.9 %while.50 = (s32[]{:T(128)}, f32[3,128]{1,0:T(4,128)S(1)}, s32[128]{0:T(128)S(1)}, s32[32,512]{1,0:T(8,128)S(1)}, f32[3,128]{1,0:T(4,128)S(1)}, /*index=5*/f32[3...) while((s32[]{:T(128)}, f32[3,128]{1,0:T(4,128)S(1)}, s32[128]{0:T(128)S(1)}, ...), condition=%wide.region_6.6_spmd.clone, body=%wide.region_1.5_spmd.clone.sunk | while | flops 2490755 | bytes 2165359 | solution.py:62
  105.9 24.9 %while.50 = (s32[]{:T(128)}, f32[3,128]{1,0:T(4,128)S(1)}, s32[128]{0:T(128)S(1)}, s32[32,512]{1,0:T(8,128)S(1)}, f32[3,128]{1,0:T(4,128)S(1)}, /*index=5*/f32[3...) while((s32[]{:T(128)}, f32[3,128]{1,0:T(4,128)S(1)}, s32[128]{0:T(128)S(1)}, ...), condition=%wide.region_6.6_spmd.clone, body=%wide.region_1.5_spmd.clone.sunk | while | flops 2490755 | bytes 2165359 | solution.py:62
  131.5 24.9 %while.50 = (s32[]{:T(128)}, f32[3,128]{1,0:T(4,128)S(1)}, s32[128]{0:T(128)S(1)}, s32[32,512]{1,0:T(8,128)S(1)}, f32[3,128]{1,0:T(4,128)S(1)}, /*index=5*/f32[3...) while((s32[]{:T(128)}, f32[3,128]{1,0:T(4,128)S(1)}, s32[128]{0:T(128)S(1)}, ...), condition=%wide.region_6.6_spmd.clone, body=%wide.region_1.5_spmd.clone.sunk | while | flops 2490755 | bytes 2165359 | solution.py:62
  157.2 24.9 %while.50 = (s32[]{:T(128)}, f32[3,128]{1,0:T(4,128)S(1)}, s32[128]{0:T(128)S(1)}, s32[32,512]{1,0:T(8,128)S(1)}, f32[3,128]{1,0:T(4,128)S(1)}, /*index=5*/f32[3...) while((s32[]{:T(128)}, f32[3,128]{1,0:T(4,128)S(1)}, s32[128]{0:T(128)S(1)}, ...), condition=%wide.region_6.6_spmd.clone, body=%wide.region_1.5_spmd.clone.sunk | while | flops 2490755 | bytes 2165359 | solution.py:62
  182.8 24.9 %while.50 = (s32[]{:T(128)}, f32[3,128]{1,0:T(4,128)S(1)}, s32[128]{0:T(128)S(1)}, s32[32,512]{1,0:T(8,128)S(1)}, f32[3,128]{1,0:T(4,128)S(1)}, /*index=5*/f32[3...) while((s32[]{:T(128)}, f32[3,128]{1,0:T(4,128)S(1)}, s32[128]{0:T(128)S(1)}, ...), condition=%wide.region_6.6_spmd.clone, body=%wide.region_1.5_spmd.clone.sunk | while | flops 2490755 | bytes 2165359 | solution.py:62
  208.4 24.9 %while.50 = (s32[]{:T(128)}, f32[3,128]{1,0:T(4,128)S(1)}, s32[128]{0:T(128)S(1)}, s32[32,512]{1,0:T(8,128)S(1)}, f32[3,128]{1,0:T(4,128)S(1)}, /*index=5*/f32[3...) while((s32[]{:T(128)}, f32[3,128]{1,0:T(4,128)S(1)}, s32[128]{0:T(128)S(1)}, ...), condition=%wide.region_6.6_spmd.clone, body=%wide.region_1.5_spmd.clone.sunk | while | flops 2490755 | bytes 2165359 | solution.py:62
  234.0 24.9 %while.50 = (s32[]{:T(128)}, f32[3,128]{1,0:T(4,128)S(1)}, s32[128]{0:T(128)S(1)}, s32[32,512]{1,0:T(8,128)S(1)}, f32[3,128]{1,0:T(4,128)S(1)}, /*index=5*/f32[3...) while((s32[]{:T(128)}, f32[3,128]{1,0:T(4,128)S(1)}, s32[128]{0:T(128)S(1)}, ...), condition=%wide.region_6.6_spmd.clone, body=%wide.region_1.5_spmd.clone.sunk | while | flops 2490755 | bytes 2165359 | solution.py:62
  258.9 18.3 %all-gather.3 = f32[16,3,1024]{2,1,0:T(4,128)S(1)} all-gather(f32[1,3,1024]{2,1,0:T(4,128)S(1)} %fusion.27), channel_id=3, replica_groups=mesh['row'=16,'col'=16] {'row'}, dimensions={0}, use_global_device_ids=true | all-gather | bytes 208896 | tf_op jit(solution)/shard_map/all_gather | solution.py:11
  277.2 204.9 %while.49 = (s32[]{:T(128)}, f32[8,3,128]{2,1,0:T(4,128)S(1)}, f32[8,3,128]{2,1,0:T(4,128)}, s32[8,128]{1,0:T(8,128)S(1)}, f32[32,3,512]{2,1,0:T(4,128)S(1)}, /*...) while((s32[]{:T(128)}, f32[8,3,128]{2,1,0:T(4,128)S(1)}, ...), condition=%wide.region_15.16_spmd.clone, body=%wide.region_8.15_spmd.clone.sunk | while | flops 2523525 | bytes 2239280 | solution.py:67
  278.0 24.9 %while.51 = (s32[]{:T(128)}, f32[3,128]{1,0:T(4,128)S(1)}, s32[128]{0:T(128)S(1)}, s32[32,512]{1,0:T(8,128)S(1)}, f32[3,128]{1,0:T(4,128)S(1)}, /*index=5*/f32[3...) while((s32[]{:T(128)}, f32[3,128]{1,0:T(4,128)S(1)}, s32[128]{0:T(128)S(1)}, ...), condition=%wide.region_14.14_spmd.clone, body=%wide.region_9.13_spmd.clone.sunk | while | flops 2490755 | bytes 2165359 | solution.py:62
  303.6 24.9 %while.51 = (s32[]{:T(128)}, f32[3,128]{1,0:T(4,128)S(1)}, s32[128]{0:T(128)S(1)}, s32[32,512]{1,0:T(8,128)S(1)}, f32[3,128]{1,0:T(4,128)S(1)}, /*index=5*/f32[3...) while((s32[]{:T(128)}, f32[3,128]{1,0:T(4,128)S(1)}, s32[128]{0:T(128)S(1)}, ...), condition=%wide.region_14.14_spmd.clone, body=%wide.region_9.13_spmd.clone.sunk | while | flops 2490755 | bytes 2165359 | solution.py:62
  329.2 24.9 %while.51 = (s32[]{:T(128)}, f32[3,128]{1,0:T(4,128)S(1)}, s32[128]{0:T(128)S(1)}, s32[32,512]{1,0:T(8,128)S(1)}, f32[3,128]{1,0:T(4,128)S(1)}, /*index=5*/f32[3...) while((s32[]{:T(128)}, f32[3,128]{1,0:T(4,128)S(1)}, s32[128]{0:T(128)S(1)}, ...), condition=%wide.region_14.14_spmd.clone, body=%wide.region_9.13_spmd.clone.sunk | while | flops 2490755 | bytes 2165359 | solution.py:62
  354.8 24.9 %while.51 = (s32[]{:T(128)}, f32[3,128]{1,0:T(4,128)S(1)}, s32[128]{0:T(128)S(1)}, s32[32,512]{1,0:T(8,128)S(1)}, f32[3,128]{1,0:T(4,128)S(1)}, /*index=5*/f32[3...) while((s32[]{:T(128)}, f32[3,128]{1,0:T(4,128)S(1)}, s32[128]{0:T(128)S(1)}, ...), condition=%wide.region_14.14_spmd.clone, body=%wide.region_9.13_spmd.clone.sunk | while | flops 2490755 | bytes 2165359 | solution.py:62
  380.4 24.9 %while.51 = (s32[]{:T(128)}, f32[3,128]{1,0:T(4,128)S(1)}, s32[128]{0:T(128)S(1)}, s32[32,512]{1,0:T(8,128)S(1)}, f32[3,128]{1,0:T(4,128)S(1)}, /*index=5*/f32[3...) while((s32[]{:T(128)}, f32[3,128]{1,0:T(4,128)S(1)}, s32[128]{0:T(128)S(1)}, ...), condition=%wide.region_14.14_spmd.clone, body=%wide.region_9.13_spmd.clone.sunk | while | flops 2490755 | bytes 2165359 | solution.py:62
  406.0 24.9 %while.51 = (s32[]{:T(128)}, f32[3,128]{1,0:T(4,128)S(1)}, s32[128]{0:T(128)S(1)}, s32[32,512]{1,0:T(8,128)S(1)}, f32[3,128]{1,0:T(4,128)S(1)}, /*index=5*/f32[3...) while((s32[]{:T(128)}, f32[3,128]{1,0:T(4,128)S(1)}, s32[128]{0:T(128)S(1)}, ...), condition=%wide.region_14.14_spmd.clone, body=%wide.region_9.13_spmd.clone.sunk | while | flops 2490755 | bytes 2165359 | solution.py:62
  431.6 24.9 %while.51 = (s32[]{:T(128)}, f32[3,128]{1,0:T(4,128)S(1)}, s32[128]{0:T(128)S(1)}, s32[32,512]{1,0:T(8,128)S(1)}, f32[3,128]{1,0:T(4,128)S(1)}, /*index=5*/f32[3...) while((s32[]{:T(128)}, f32[3,128]{1,0:T(4,128)S(1)}, s32[128]{0:T(128)S(1)}, ...), condition=%wide.region_14.14_spmd.clone, body=%wide.region_9.13_spmd.clone.sunk | while | flops 2490755 | bytes 2165359 | solution.py:62
  457.2 24.9 %while.51 = (s32[]{:T(128)}, f32[3,128]{1,0:T(4,128)S(1)}, s32[128]{0:T(128)S(1)}, s32[32,512]{1,0:T(8,128)S(1)}, f32[3,128]{1,0:T(4,128)S(1)}, /*index=5*/f32[3...) while((s32[]{:T(128)}, f32[3,128]{1,0:T(4,128)S(1)}, s32[128]{0:T(128)S(1)}, ...), condition=%wide.region_14.14_spmd.clone, body=%wide.region_9.13_spmd.clone.sunk | while | flops 2490755 | bytes 2165359 | solution.py:62
  483.3 27.7 %gather_fusion.1 = f32[8192,9]{1,0:T(8,128)} fusion(f32[9,1024]{0,1:T(8,128)S(1)} %copy.32, s32[8192]{0:T(1024)S(1)} %broadcast_clamp_fusion), kind=kCustom, calls=%fused_computation.1.clone | custom fusion | bytes 622592 | tf_op jit(solution)/shard_map/jit(_take)/gather | solution.py:122
  511.0 2.8 copy.35
  514.7 9.5 %all-to-all-start.1 = ((f32[9,16,512]{2,0,1:T(8,128)}), f32[9,16,512]{2,0,1:T(8,128)S(1)}, u32[]{:S(2)}, u32[]{:S(2)}) async-start(f32[9,16,512]{2,0,1:T(8,128)} %select_bitcast_fusion), calls=%async_computation.1 | async-start | bytes 1048576 | tf_op jit(solution)/shard_map/all_to_all | solution.py:123
  524.3 27.7 %gather_fusion = f32[8192,9]{1,0:T(8,128)} fusion(f32[9,1024]{0,1:T(8,128)S(1)} %copy.32, s32[8192]{0:T(1024)S(1)} %broadcast_clamp_fusion.1), kind=kCustom, calls=%fused_computation.clone | custom fusion | bytes 622592 | tf_op jit(solution)/shard_map/jit(_take)/gather | solution.py:120
  552.0 2.8 copy.33
  556.4 9.1 %all-to-all-start.2 = ((f32[3,16,512]{2,0,1:T(4,128)}), f32[3,16,512]{2,0,1:T(4,128)S(1)}, u32[]{:S(2)}, u32[]{:S(2)}) async-start(f32[3,16,512]{2,0,1:T(4,128)} %add_multiply_fusion), calls=%async_computation.2 | async-start | bytes 262144 | tf_op jit(solution)/shard_map/all_to_all | solution.py:127
  565.5 3.4 copy.36
  569.0 44.4 %scatter_custom_fusion = f32[3,1024]{0,1:T(8,128)S(1)} fusion(s32[8192]{0:T(1024)S(1)} %bitcast.130, f32[8192,3]{1,0:T(8,128)} %copy.36, f32[]{:T(128)} %constant.84.clone.1), kind=kCustom, calls=%fused_computation.54 | custom fusion | flops 24576 | bytes 12800 | tf_op jit(solution)/shard_map/scatter-add | solution.py:94
  613.4 2.6 copy.37
  616.0 44.4 %scatter_custom_fusion.1 = f32[3,1024]{0,1:T(8,128)S(1)} fusion(s32[8192]{0:T(1024)S(1)} %bitcast.131, f32[8192,3]{1,0:T(8,128)} %copy.37, f32[]{:T(128)} %constant.84.clone.1), kind=kCustom, calls=%fused_computation.52 | custom fusion | flops 24576 | bytes 12800 | tf_op jit(solution)/shard_map/scatter-add | solution.py:94
  (3709 shorter events, 392.6 us)
Async XLA Ops:
  2.0 481.2 %all-to-all-start = ((s32[16,1,512]{2,1,0:T(1,128)}), s32[16,1,512]{2,1,0:T(1,128)S(1)}, u32[]{:S(2)}, u32[]{:S(2)}) async-start(s32[16,1,512]{2,1,0:T(1,128)} %all_to_all.14), calls=%async_computation | async-start | bytes 65536 | tf_op jit(solution)/shard_map/all_to_all | solution.py:121
  54.0 204.9 %copy-start.1 = (f32[3,1024]{1,0:T(4,128)S(1)}, f32[3,1024]{1,0:T(4,128)}, u32[]{:S(2)}) copy-start(f32[3,1024]{1,0:T(4,128)} %param.19) | copy-start | bytes 36868
  54.0 204.9 %copy-start.3 = (f32[1024]{0:T(1024)S(1)}, f32[1024]{0:T(1024)}, u32[]{:S(2)}) copy-start(f32[1024]{0:T(1024)} %param.20) | copy-start | bytes 12292
  277.2 205.0 %copy-start.4 = (f32[3,1024]{1,0:T(4,128)S(1)}, f32[3,1024]{1,0:T(4,128)}, u32[]{:S(2)}) copy-start(f32[3,1024]{1,0:T(4,128)} %param.18) | copy-start | bytes 36868
  482.1 31.7 %copy-start.2 = (f32[3,1024]{1,0:T(4,128)}, f32[3,1024]{1,0:T(4,128)S(1)}, u32[]{:S(2)}) copy-start(f32[3,1024]{1,0:T(4,128)S(1)} %fusion.25) | copy-start | bytes 36868
  483.3 40.9 %copy-start.5 = (s32[1,1,16]{2,1,0:T(1,128)S(1)}, s32[1,1,16]{2,1,0:T(1,128)}, u32[]{:S(2)}) copy-start(s32[1,1,16]{2,1,0:T(1,128)} %param.23) | copy-start | bytes 196
  514.7 40.1 %copy-start = (s32[1,1,16,512]{3,2,1,0:T(8,128)S(1)}, s32[1,1,16,512]{3,2,1,0:T(8,128)}, u32[]{:S(2)}) copy-start(s32[1,1,16,512]{3,2,1,0:T(8,128)} %param.21) | copy-start | bytes 98308
  514.7 40.2 %all-to-all-start.1 = ((f32[9,16,512]{2,0,1:T(8,128)}), f32[9,16,512]{2,0,1:T(8,128)S(1)}, u32[]{:S(2)}, u32[]{:S(2)}) async-start(f32[9,16,512]{2,0,1:T(8,128)} %select_bitcast_fusion), calls=%async_computation.1 | async-start | bytes 1048576 | tf_op jit(solution)/shard_map/all_to_all | solution.py:123
  556.4 57.0 %all-to-all-start.2 = ((f32[3,16,512]{2,0,1:T(4,128)}), f32[3,16,512]{2,0,1:T(4,128)S(1)}, u32[]{:S(2)}, u32[]{:S(2)}) async-start(f32[3,16,512]{2,0,1:T(4,128)} %add_multiply_fusion), calls=%async_computation.2 | async-start | bytes 262144 | tf_op jit(solution)/shard_map/all_to_all | solution.py:127
